TPU v7x, 32 devices: a whole 2x2x4 slice. The times are simulated.
32 devices in a mesh: phi: 4 (over y, core), eta: 8 (over z, x).
Axes of the slice: x: 2, y: 2, z: 4, core: 2. Of those that a mesh axis runs over, the one named last changes fastest.
Arguments:
- edges: bfloat16 [65536, 128], P(('phi', 'eta')), may hold values from -6 to 6
- cotangent: bfloat16 [65536, 128], P(('phi', 'eta')), may hold values from -6 to 6
- send_rows: int32 [32, 32, 32], P(('phi', 'eta')), may hold values from 0 to 2047
- send_count: int32 [32, 32], P(('phi', 'eta')), may hold values from 1 to 32, as said below
- trip_local: int32 [262144], P(('phi', 'eta')), may hold values from 0 to 2047
- trip_remote: int32 [262144], P(('phi', 'eta')), may hold values from 0 to 1023, as said below
- w_first: bfloat16 [384, 256], replicated, may hold values from -0.3125 to 0.3125
- bias_first: float32 [256], replicated, may hold values from -4 to 4
- w_second: bfloat16 [256, 128], replicated, may hold values from -0.375 to 0.375
Outputs:
- new_edges: bfloat16 [65536, 128], P(('phi', 'eta'))
- edge_grad: bfloat16 [65536, 128], P(('phi', 'eta'))
- grad_first: float32 [384, 256], replicated
- grad_bias: float32 [256], replicated
- grad_second: float32 [256, 128], replicated
Inputs may be any that keep to these rules, and one draw needn't show every extreme that they name: `send_count`: some destination device has every slot live from every source. `trip_remote`: each triplet names a live slot of a source device toward its own owner.
All inputs are finite; a program needn't handle non-finite values.
Results may differ from a plain program's by a relative error of at most 0.0053.
Values may be sent and summed in bfloat16 or wider, within the bound.
A program may use at most 128 MiB of HBM per device.

v0:
```python
import jax
import jax.numpy as jnp
from jax import lax
from jax.sharding import PartitionSpec as P


def silu_slope(pre):
    sig = jax.nn.sigmoid(pre)
    return sig * (1.0 + pre * (1.0 - sig))


def local(
    edges, cotangent, send_rows, send_count, trip_local, trip_remote, w_first, bias_first, w_second
):
    width = edges.shape[1]
    local_edges = edges.shape[0]
    n_phi = lax.axis_size("phi")
    n_eta = lax.axis_size("eta")
    ndev = n_phi * n_eta
    slots_per = send_rows.shape[2]
    rows = send_rows[0]
    live = jnp.arange(slots_per, dtype=jnp.int32)[None, :] < send_count[0][:, None]
    zero = jnp.zeros((), jnp.bfloat16)
    stacked = jnp.stack([edges, cotangent], axis=1)
    outgoing = jnp.where(live[:, :, None, None], stacked[rows], zero)
    arrived = lax.all_to_all(outgoing, ("phi", "eta"), split_axis=0, concat_axis=0, tiled=True)
    arrived = arrived.reshape(ndev * slots_per, 2, width)
    inner = edges[trip_local]
    inner_cot = cotangent[trip_local]
    outer_pair = arrived[trip_remote]
    outer = outer_pair[:, 0, :]
    outer_cot = outer_pair[:, 1, :]
    inner_f = inner.astype(jnp.float32)
    outer_f = outer.astype(jnp.float32)
    prod = (inner_f * outer_f).astype(jnp.bfloat16)
    joined = jnp.concatenate([inner, outer, prod], axis=1)
    pre = jnp.dot(joined, w_first, preferred_element_type=jnp.float32) + bias_first
    hidden = jax.nn.silu(pre).astype(jnp.bfloat16)
    message = jnp.dot(hidden, w_second, preferred_element_type=jnp.float32)
    dmsg = (inner_cot.astype(jnp.float32) + outer_cot.astype(jnp.float32)).astype(jnp.bfloat16)
    dpre = jnp.dot(dmsg, w_second.T, preferred_element_type=jnp.float32) * silu_slope(pre)
    dpre_b = dpre.astype(jnp.bfloat16)
    dx = jnp.dot(dpre_b, w_first.T, preferred_element_type=jnp.float32)
    d_inner = dx[:, :width] + dx[:, 2 * width :] * outer_f
    d_outer = dx[:, width : 2 * width] + dx[:, 2 * width :] * inner_f
    slot_msg = jax.ops.segment_sum(message, trip_remote, ndev * slots_per)
    slot_grad = jax.ops.segment_sum(d_outer, trip_remote, ndev * slots_per)
    slot_sums = (
        jnp.stack([slot_msg, slot_grad], axis=1)
        .astype(jnp.bfloat16)
        .reshape(ndev, slots_per, 2, width)
    )
    returned = lax.all_to_all(slot_sums, ("phi", "eta"), split_axis=0, concat_axis=0, tiled=True)
    returned = jnp.where(live[:, :, None, None], returned, zero)
    grad_second = jnp.dot(hidden.T, dmsg, preferred_element_type=jnp.float32)
    grad_first = jnp.dot(joined.T, dpre_b, preferred_element_type=jnp.float32)
    grad_bias = jnp.sum(dpre, axis=0)
    grad_first, grad_bias, grad_second = lax.psum(
        (grad_first, grad_bias, grad_second), ("phi", "eta")
    )
    local_msg = jax.ops.segment_sum(message, trip_local, local_edges)
    local_grad = jax.ops.segment_sum(d_inner, trip_local, local_edges)
    flat_rows = rows.reshape(-1)
    local_msg = local_msg.at[flat_rows].add(
        returned[:, :, 0, :].astype(jnp.float32).reshape(-1, width)
    )
    local_grad = local_grad.at[flat_rows].add(
        returned[:, :, 1, :].astype(jnp.float32).reshape(-1, width)
    )
    new_edges = (edges.astype(jnp.float32) + local_msg).astype(jnp.bfloat16)
    edge_grad = (cotangent.astype(jnp.float32) + local_grad).astype(jnp.bfloat16)
    return (new_edges, edge_grad, grad_first, grad_bias, grad_second)


def solution(mesh):
    in_specs = (
        P(("phi", "eta"), None),
        P(("phi", "eta"), None),
        P(("phi", "eta"), None, None),
        P(("phi", "eta"), None),
        P(("phi", "eta")),
        P(("phi", "eta")),
        P(),
        P(),
        P(),
    )
    out_specs = (P(("phi", "eta"), None), P(("phi", "eta"), None), P(), P(), P())
    return jax.shard_map(local, mesh=mesh, in_specs=in_specs, out_specs=out_specs, check_vma=False)
```

profile of v0, /device:TPU:0, one launch (start us, length us, event | category | flops | bytes accessed | tf_op | source)
XLA Modules:
  0.0 520.3 jit_solution(7421459561959832188)
XLA Ops:
  7.2 0.0 copy-start
  7.2 0.8 iota_compare_fusion
  8.0 0.7 compare_select_fusion.2
  8.7 0.1 reshape.125
  8.8 1.8 copy.21
  10.6 0.0 copy-start.11
  10.6 0.0 copy-start.2
  10.6 1.9 copy.20
  12.4 0.0 copy-start.3
  12.5 0.0 copy-start.9
  12.5 2.4 pad_maximum_fusion.3
  14.9 3.7 gather_fusion.1
  18.6 1.0 copy_select_fusion
  19.6 7.3 %all-to-all-start = ((bf16[32,32,2,128]{3,1,2,0:T(8,128)(2,1)}), bf16[32,32,2,128]{3,1,2,0:T(8,128)(2,1)S(1)}, u32[]{:S(2)}, u32[]{:S(2)}) async-start(bf16[32,32,2,128]{3,1,2,0:T(8,128)(2,1)} %copy_select_fusion), calls=%async_computation | async-start | bytes 1048576 | tf_op jit(solution)/shard_map/all_to_all | solution.py:26
  26.9 0.0 copy-done.11
  26.9 0.1 reshape_squeeze.3
  27.0 0.0 copy-done.2
  27.0 0.1 convert_element_type.55
  27.1 0.0 copy-done.3
  27.1 1.1 convert_element_type.68
  28.2 0.0 copy-done.9
  28.2 29.2 %gather_fusion = bf16[8192,128]{1,0:T(8,128)(2,1)} fusion(bf16[2048,128]{1,0:T(8,128)(2,1)S(1)} %copy-done.2, s32[8192]{0:T(1024)S(1)} %fusion.22), kind=kCustom, calls=%fused_computation | custom fusion | bytes 4227072 | tf_op jit(solution)/shard_map/gather | solution.py:28
  57.4 29.2 %gather_fusion.3 = bf16[8192,128]{1,0:T(8,128)(2,1)} fusion(bf16[2048,128]{1,0:T(8,128)(2,1)S(1)} %copy-done.3, s32[8192]{0:T(1024)S(1)} %fusion.22), kind=kCustom, calls=%fused_computation.3 | custom fusion | bytes 4227072 | tf_op jit(solution)/shard_map/gather | solution.py:29
  86.6 0.0 copy-done.12
  86.7 0.0 all-to-all-done
  86.7 0.5 copy.23
  87.2 53.3 %gather_fusion.2 = bf16[8192,2,128]{2,1,0:T(2,128)(2,1)} fusion(bf16[1024,2,128]{2,1,0:T(2,128)(2,1)S(1)} %bitcast.30, s32[8192]{0:T(1024)S(1)} %fusion.23), kind=kCustom, calls=%fused_computation.2 | custom fusion | bytes 8421376 | tf_op jit(solution)/shard_map/gather | solution.py:30
  140.5 9.5 %slice_convert_fusion = (f32[8192,1,128]{2,1,0:T(1,128)}, bf16[8192,1,128]{2,1,0:T(2,128)(2,1)S(1)}) fusion(bf16[8192,2,128]{2,1,0:T(2,128)(2,1)} %gather_fusion.2), kind=kLoop, calls=%fused_computation.25 | loop fusion | flops 1048576 | bytes 10485760 | tf_op jit(solution)/shard_map/convert_element_type | solution.py:40
  150.1 0.8 fusion.3
  150.9 0.0 copy-start.6
  150.9 0.0 copy-start.8
  150.9 0.0 copy-done
  150.9 0.0 copy-done.13
  150.9 0.0 copy-start.10
  150.9 5.2 %multiply_convert_fusion = (bf16[8192,256]{1,0:T(8,128)(2,1)S(1)}, f32[8192,256]{1,0:T(8,128)}) fusion(f32[256]{0:T(256)S(1)} %copy-done.13, bf16[384,256]{1,0:T(8,128)(2,1)S(1)} %copy-done, bf16[8192,128]{1,0:T(8,128)(2,1)S(1)} %get-tuple-element.7, bf16[8192,128]{1,0:T(8,128)(2,1)S(1)} %get-tuple-element.8, bf16[8192,128]{1,0:T(8,128)(2,1)S(1)} %copy-done.5), kind=kOutput, calls=%fused_computation.12 | convolution fusion | flops 1642070016 | bytes 19072000 | tf_op jit(solution)/shard_map/dot_general | solution.py:37
  156.1 2.0 copy-done.4
  158.1 3.2 fusion.29
  161.3 45.1 %scatter_custom_fusion.1 = f32[1024,128]{1,0:T(8,128)} fusion(s32[8192]{0:T(1024)S(1)} %copy-done.12, f32[8192,128]{1,0:T(8,128)} %fusion.29, f32[]{:T(128)} %constant.11.clone.1), kind=kCustom, calls=%fused_computation.43 | custom fusion | flops 1048576 | bytes 524800 | tf_op jit(solution)/shard_map/scatter-add | solution.py:46
  206.4 1.8 convert.11
  208.2 7.9 %fusion.28 = (f32[256]{0:T(256)S(1)}, bf16[8192,256]{1,0:T(8,128)(2,1)S(1)}) fusion(f32[8192,256]{1,0:T(8,128)} %get-tuple-element.14, bf16[256,128]{1,0:T(8,128)(2,1)S(1)} %copy-done.10, f32[8192,128]{1,0:T(8,128)} %bitcast.31, bf16[8192,128]{1,0:T(8,128)(2,1)} %gather_fusion.3), kind=kOutput, calls=%fused_computation.57 | convolution fusion | flops 560987904 | bytes 18940928 | tf_op jit(solution)/shard_map/dot_general | solution.py:41
  216.1 1.9 copy-done.7
  218.0 6.9 %fusion.13 = f32[8192,384]{1,0:T(8,128)} fusion(bf16[384,256]{1,0:T(8,128)(2,1)S(1)} %copy-done, bf16[8192,256]{1,0:T(8,128)(2,1)S(1)} %get-tuple-element.16), kind=kOutput, calls=%fused_computation.32 | convolution fusion | flops 1610612736 | bytes 16973824 | tf_op jit(solution)/shard_map/dot_general | solution.py:43
  225.0 45.7 %scatter_custom_fusion.2 = f32[1024,128]{1,0:T(8,128)} fusion(s32[8192]{0:T(1024)S(1)} %copy-done.12, bf16[8192,128]{1,0:T(8,128)(2,1)S(1)} %copy-done.5, f32[8192,384]{1,0:T(8,128)} %fusion.13, f32[]{:T(128)} %constant.11.clone.1), kind=kCustom, calls=%fused_computation.19 | custom fusion | flops 4194304 | bytes 11010560 | tf_op jit(solution)/shard_map/scatter-add | solution.py:47
  270.7 1.1 convert.12
  271.8 1.0 pad_maximum_fusion.4
  272.8 0.9 copy.25
  273.6 6.0 %all-to-all-start.1 = ((bf16[32,32,2,128]{3,1,2,0:T(8,128)(2,1)}), bf16[32,32,2,128]{3,1,2,0:T(8,128)(2,1)}, u32[]{:S(2)}, u32[]{:S(2)}) async-start(bf16[32,32,2,128]{3,1,2,0:T(8,128)(2,1)} %copy.25), calls=%async_computation.1 | async-start | bytes 1048576 | tf_op jit(solution)/shard_map/all_to_all | solution.py:53
  279.6 0.0 all-reduce.3.cloned.1.call-start
  279.6 6.0 %fusion.26 = f32[256,128]{1,0:T(8,128)} fusion(bf16[8192,256]{1,0:T(8,128)(2,1)} %copy-done.4, f32[8192,128]{1,0:T(8,128)} %bitcast.32, bf16[8192,128]{1,0:T(8,128)(2,1)} %gather_fusion.3), kind=kOutput, calls=%fused_computation.55 | convolution fusion | flops 540016640 | bytes 10616832 | tf_op jit(solution)/shard_map/dot_general | solution.py:55
  285.7 44.7 %scatter_fusion = f32[2048,128]{1,0:T(8,128)S(1)} fusion(f32[2048,128]{1,0:T(8,128)S(1)} %convert_element_type.55, s32[8192]{0:T(1024)S(1)} %copy-done.9, f32[8192,128]{1,0:T(8,128)} %fusion.29), kind=kCustom, calls=%fused_computation.4 | custom fusion | flops 1048576 | bytes 12615680 | tf_op jit(solution)/shard_map/scatter-add | solution.py:61
  330.4 42.8 %scatter_custom_fusion.4 = f32[2048,128]{1,0:T(8,128)} fusion(f32[2048,128]{1,0:T(8,128)} %convert_element_type.68, s32[8192]{0:T(1024)S(1)} %copy-done.9, bf16[8192,128]{1,0:T(8,128)(2,1)} %copy-done.6, f32[8192,384]{1,0:T(8,128)} %fusion.13), kind=kCustom, calls=%fused_computation.22 | custom fusion | flops 4194304 | bytes 11534336 | tf_op jit(solution)/shard_map/scatter-add | solution.py:62
  373.2 6.0 %fusion.11 = f32[384,256]{1,0:T(8,128)} fusion(bf16[8192,128]{1,0:T(8,128)(2,1)} %copy-done.8, bf16[8192,128]{1,0:T(8,128)(2,1)} %copy-done.6, bf16[8192,128]{1,0:T(8,128)(2,1)S(1)} %copy-done.5, bf16[8192,256]{1,0:T(8,128)(2,1)} %copy-done.7), kind=kOutput, calls=%fused_computation.29 | convolution fusion | flops 1629487104 | bytes 10878976 | tf_op jit(solution)/shard_map/dot_general | solution.py:56
  379.2 0.0 all-reduce.3.cloned.1.call-update
  379.2 40.6 %psum.22 = f32[256]{0:T(256)} all-reduce(f32[256]{0:T(256)S(1)} %get-tuple-element.15), channel_id=1, replica_groups=mesh['phi'=4,'eta'=8] {'phi','eta'}, use_global_device_ids=true, to_apply=%region_8.9 | all-reduce | flops 256 | bytes 2048 | tf_op jit(solution)/shard_map/psum | solution.py:58
  419.8 0.0 all-to-all-done.1
  419.8 1.3 broadcast_select_fusion
  421.2 7.7 %scatter_custom_fusion.5 = f32[2048,128]{1,0:T(8,128)} fusion(f32[2048,128]{1,0:T(8,128)} %scatter_custom_fusion.4, s32[1024]{0:T(1024)S(1)} %bitcast.38, bf16[1024,128]{1,0:T(8,128)(2,1)S(1)} %bitcast.36), kind=kCustom, calls=%fused_computation.36 | custom fusion | flops 262144 | bytes 1310720 | tf_op jit(solution)/shard_map/scatter-add | solution.py:67
  428.8 2.1 convert_element_type.71
  430.9 6.5 %scatter_custom_fusion.3 = f32[2048,128]{1,0:T(8,128)S(1)} fusion(f32[2048,128]{1,0:T(8,128)S(1)} %scatter_fusion, s32[1024]{0:T(1024)S(1)} %bitcast.39, bf16[1024,128]{1,0:T(8,128)(2,1)S(1)} %bitcast.35), kind=kCustom, calls=%fused_computation.38 | custom fusion | flops 262144 | bytes 1310720 | tf_op jit(solution)/shard_map/scatter-add | solution.py:64
  437.4 0.8 convert_element_type.67
  438.2 71.9 %all-reduce.3.cloned.1.call-done = (f32[384,256]{1,0:T(8,128)}, f32[256,128]{1,0:T(8,128)}) async-done(((f32[384,256]{1,0:T(8,128)}, f32[256,128]{1,0:T(8,128)}), (f32[384,256]{1,0:T(8,128)}, f32[256,128]{1,0:T(8,128)})) %all-reduce.3.cloned.1.call-update) | async-done | bytes 524304 | tf_op jit(solution)/shard_map/psum | solution.py:58
  510.1 1.8 copy.36
  511.9 1.6 copy.37
  513.4 0.0 copy-done.1
  (15 shorter events, 0.1 us)
Async XLA Ops:
  7.2 143.7 %copy-start = (bf16[384,256]{1,0:T(8,128)(2,1)S(1)}, bf16[384,256]{1,0:T(8,128)(2,1)}, u32[]{:S(2)}) copy-start(bf16[384,256]{1,0:T(8,128)(2,1)} %param.15) | copy-start | bytes 589828
  10.6 16.4 %copy-start.11 = (s32[1,32,32]{2,1,0:T(8,128)S(1)}, s32[1,32,32]{2,1,0:T(8,128)}, u32[]{:S(2)}) copy-start(s32[1,32,32]{2,1,0:T(8,128)} %param.11) | copy-start | bytes 12292
  10.6 16.5 %copy-start.2 = (bf16[2048,128]{1,0:T(8,128)(2,1)S(1)}, bf16[2048,128]{1,0:T(8,128)(2,1)}, u32[]{:S(2)}) copy-start(bf16[2048,128]{1,0:T(8,128)(2,1)} %param.9) | copy-start | bytes 1572868
  12.4 14.7 %copy-start.3 = (bf16[2048,128]{1,0:T(8,128)(2,1)S(1)}, bf16[2048,128]{1,0:T(8,128)(2,1)}, u32[]{:S(2)}) copy-start(bf16[2048,128]{1,0:T(8,128)(2,1)} %param.10) | copy-start | bytes 1572868
  12.5 15.7 %copy-start.9 = (s32[8192]{0:T(1024)S(1)}, s32[8192]{0:T(1024)}, u32[]{:S(2)}) copy-start(s32[8192]{0:T(1024)} %param.13) | copy-start | bytes 98308
  19.6 67.1 %all-to-all-start = ((bf16[32,32,2,128]{3,1,2,0:T(8,128)(2,1)}), bf16[32,32,2,128]{3,1,2,0:T(8,128)(2,1)S(1)}, u32[]{:S(2)}, u32[]{:S(2)}) async-start(bf16[32,32,2,128]{3,1,2,0:T(8,128)(2,1)} %copy_select_fusion), calls=%async_computation | async-start | bytes 1048576 | tf_op jit(solution)/shard_map/all_to_all | solution.py:26
  57.4 29.2 %copy-start.12 = (s32[8192]{0:T(1024)S(1)}, s32[8192]{0:T(1024)}, u32[]{:S(2)}) copy-start(s32[8192]{0:T(1024)} %param.14) | copy-start | bytes 98308
  140.5 9.5 %copy-start.5 = (bf16[8192,128]{1,0:T(8,128)(2,1)S(1)}, bf16[8192,128]{1,0:T(8,128)(2,1)}, u32[]{:S(2)}) copy-start(bf16[8192,128]{1,0:T(8,128)(2,1)} %gather_fusion) | copy-start | bytes 6291460
  150.1 0.9 copy-start.13
  150.9 5.3 %copy-start.6 = (bf16[8192,128]{1,0:T(8,128)(2,1)}, bf16[8192,128]{1,0:T(8,128)(2,1)S(1)}, u32[]{:S(2)}) copy-start(bf16[8192,128]{1,0:T(8,128)(2,1)S(1)} %get-tuple-element.8) | copy-start | bytes 6291460
  150.9 5.3 %copy-start.8 = (bf16[8192,128]{1,0:T(8,128)(2,1)}, bf16[8192,128]{1,0:T(8,128)(2,1)S(1)}, u32[]{:S(2)}) copy-start(bf16[8192,128]{1,0:T(8,128)(2,1)S(1)} %get-tuple-element.7) | copy-start | bytes 6291460
  150.9 7.2 %copy-start.10 = (bf16[256,128]{1,0:T(8,128)(2,1)S(1)}, bf16[256,128]{1,0:T(8,128)(2,1)}, u32[]{:S(2)}) copy-start(bf16[256,128]{1,0:T(8,128)(2,1)} %param.17) | copy-start | bytes 196612
  156.1 2.0 copy-start.4
  216.1 1.9 copy-start.7
  273.6 146.2 %all-to-all-start.1 = ((bf16[32,32,2,128]{3,1,2,0:T(8,128)(2,1)}), bf16[32,32,2,128]{3,1,2,0:T(8,128)(2,1)}, u32[]{:S(2)}, u32[]{:S(2)}) async-start(bf16[32,32,2,128]{3,1,2,0:T(8,128)(2,1)} %copy.25), calls=%async_computation.1 | async-start | bytes 1048576 | tf_op jit(solution)/shard_map/all_to_all | solution.py:53
  279.6 230.5 %all-reduce.3.cloned.1.call-start = ((), (), s32[]{:S(2)}) async-start(), calls=%async_computation.2 | async-start | bytes 1048576 | tf_op jit(solution)/shard_map/psum | solution.py:58
  419.8 93.6 %copy-start.1 = (bf16[384,256]{1,0:T(8,128)(2,1)S(1)}, bf16[384,256]{1,0:T(8,128)(2,1)}, u32[]{:S(2)}) copy-start(bf16[384,256]{1,0:T(8,128)(2,1)} %param.15) | copy-start | bytes 589828
Sparse Core Ops, SparseCore 0:
  379.4 130.6 all-reduce.2
where the time goes:
time: 521 us; the launch traced here: 520 us
  other arithmetic  217 us (42%)
  local copies, waits for them, and re-layouts  128 us (25%)
  waiting for transfers between devices  71.9 us (14%)
  blocking collectives  40.6 us (8%)
  matrix products  35.3 us (7%)
  between operations  14.3 us (3%)
  starting transfers between devices  13.3 us (3%)
    psum x1, waiting for transfers between devices, local(): lax.psum((grad_first, grad_bias, grad_second), ('phi', 'eta'))  71.9 us
    gather x1, local copies, waits for them, and re-layouts, local(): outer_pair = arrived[trip_remote]  53.3 us
    scatter-add x1, other arithmetic, local(): slot_grad = jax.ops.segment_sum(d_outer, trip_remote, ndev * slots_per)  45.7 us
    scatter-add x1, other arithmetic, local(): slot_msg = jax.ops.segment_sum(message, trip_remote, ndev * slots_per)  45.1 us
    scatter-add x1, other arithmetic, local(): local_msg = jax.ops.segment_sum(message, trip_local, local_edges)  44.7 us
    scatter-add x1, other arithmetic, local(): local_grad = jax.ops.segment_sum(d_inner, trip_local, local_edges)  42.8 us
    psum x1, blocking collectives, local(): lax.psum((grad_first, grad_bias, grad_second), ('phi', 'eta'))  40.6 us
    gather x1, local copies, waits for them, and re-layouts, local(): inner_cot = cotangent[trip_local]  29.2 us
  transfers between devices with their start and end apart: 3, of which 1 were waited for; matrix products, arithmetic and copies ran while one was open for 34% of the time, Pallas kernels for 0%

commit v1 on v0

--- a/solution.py
+++ b/solution.py
@@ -2,6 +2,13 @@
 import jax.numpy as jnp
 from jax import lax
 from jax.sharding import PartitionSpec as P
+from jax.lax import psum
+
+
+def side_close(incoming_x):
+    r1 = psum(incoming_x, "eta")
+    main = psum(r1, "phi")
+    return main
 
 
 def silu_slope(pre):
@@ -55,9 +62,7 @@
     grad_second = jnp.dot(hidden.T, dmsg, preferred_element_type=jnp.float32)
     grad_first = jnp.dot(joined.T, dpre_b, preferred_element_type=jnp.float32)
     grad_bias = jnp.sum(dpre, axis=0)
-    grad_first, grad_bias, grad_second = lax.psum(
-        (grad_first, grad_bias, grad_second), ("phi", "eta")
-    )
+    grad_first, grad_bias, grad_second = side_close((grad_first, grad_bias, grad_second))
     local_msg = jax.ops.segment_sum(message, trip_local, local_edges)
     local_grad = jax.ops.segment_sum(d_inner, trip_local, local_edges)
     flat_rows = rows.reshape(-1)

time: 521 us -> 441 us (0.85)
  waiting for transfers between devices: 71.9 us -> 15.2 us
  blocking collectives: 40.6 us -> 27.8 us
  matrix products: 35.3 us -> 28.4 us
    psum x1 -> x2, waiting for transfers between devices: 71.9 us -> 15.2 us  [the longest x1 15.2 us: side_close(): main = psum(r1, 'phi')]
    psum x1 -> x2, blocking collectives: 40.6 us -> 27.8 us  [the longest x1 21.6 us: side_close(): r1 = psum(incoming_x, 'eta')]
  transfers between devices with their start and end apart: 3 -> 4, of which waited for: 1 -> 1; matrix products, arithmetic and copies ran while one was open for 34% -> 39% of each run, Pallas kernels for 0% -> 0%
where the time goes in v1:
time: 441 us
  other arithmetic  216 us (49%)
  local copies, waits for them, and re-layouts  125 us (28%)
  matrix products  28.4 us (6%)
  blocking collectives  27.8 us (6%)
  waiting for transfers between devices  15.2 us (3%)
  between operations  14.4 us (3%)
  starting transfers between devices  13.4 us (3%)
    gather x1, local copies, waits for them, and re-layouts, local(): outer_pair = arrived[trip_remote]  53.2 us
    scatter-add x1, other arithmetic, local(): slot_grad = jax.ops.segment_sum(d_outer, trip_remote, ndev * slots_per)  45.7 us
    scatter-add x1, other arithmetic, local(): local_grad = jax.ops.segment_sum(d_inner, trip_local, local_edges)  45.5 us
    scatter-add x1, other arithmetic, local(): slot_msg = jax.ops.segment_sum(message, trip_remote, ndev * slots_per)  45.2 us
    scatter-add x1, other arithmetic, local(): local_msg = jax.ops.segment_sum(message, trip_local, local_edges)  44.7 us
    gather x1, local copies, waits for them, and re-layouts, local(): inner = edges[trip_local]  29.2 us
    gather x1, local copies, waits for them, and re-layouts, local(): inner_cot = cotangent[trip_local]  29.2 us
    psum x1, blocking collectives, side_close(): r1 = psum(incoming_x, 'eta')  21.6 us
  transfers between devices with their start and end apart: 4, of which 1 were waited for; matrix products, arithmetic and copies ran while one was open for 39% of the time, Pallas kernels for 0%

profile of v1, /device:TPU:0, one launch (start us, length us, event | category | flops | bytes accessed | tf_op | source)
XLA Modules:
  0.0 440.6 jit_solution(13191205977555992116)
XLA Ops:
  7.2 0.0 copy-start
  7.2 0.8 iota_compare_fusion
  7.9 1.8 copy.20
  9.7 0.0 copy-start.8
  9.8 0.0 copy-start.2
  9.8 1.9 copy.21
  11.6 0.7 compare_select_fusion.2
  12.4 0.1 reshape.125
  12.4 3.2 pad_maximum_fusion.3
  15.6 4.9 %gather_fusion.1 = bf16[1024,2,128]{2,1,0:T(2,128)(2,1)S(1)} fusion(bf16[2048,2,128]{2,1,0:T(2,128)(2,1)} %pad_maximum_fusion.3, s32[1024]{0:T(1024)S(1)} %broadcast_clamp_fusion), kind=kCustom, calls=%fused_computation.1 | custom fusion | bytes 1052672 | tf_op jit(solution)/shard_map/gather | solution.py:32
  20.6 1.0 copy_select_fusion
  21.6 7.5 %all-to-all-start = ((bf16[32,32,2,128]{3,1,2,0:T(8,128)(2,1)}), bf16[32,32,2,128]{3,1,2,0:T(8,128)(2,1)S(1)}, u32[]{:S(2)}, u32[]{:S(2)}) async-start(bf16[32,32,2,128]{3,1,2,0:T(8,128)(2,1)} %copy_select_fusion), calls=%async_computation | async-start | bytes 1048576 | tf_op jit(solution)/shard_map/all_to_all | solution.py:33
  29.1 0.0 copy-done.8
  29.1 0.0 copy-done.2
  29.1 0.0 copy-start.1
  29.1 29.2 %gather_fusion = bf16[8192,128]{1,0:T(8,128)(2,1)} fusion(bf16[2048,128]{1,0:T(8,128)(2,1)S(1)} %copy-done.2, s32[8192]{0:T(1024)S(1)} %fusion.22), kind=kCustom, calls=%fused_computation | custom fusion | bytes 4227072 | tf_op jit(solution)/shard_map/gather | solution.py:35
  58.3 0.0 copy-done.1
  58.3 29.2 %gather_fusion.3 = bf16[8192,128]{1,0:T(8,128)(2,1)} fusion(bf16[2048,128]{1,0:T(8,128)(2,1)S(1)} %copy-done.1, s32[8192]{0:T(1024)S(1)} %fusion.22), kind=kCustom, calls=%fused_computation.3 | custom fusion | bytes 4227072 | tf_op jit(solution)/shard_map/gather | solution.py:36
  87.5 0.0 copy-done.11
  87.5 0.0 all-to-all-done
  87.6 0.5 copy.23
  88.1 53.2 %gather_fusion.2 = bf16[8192,2,128]{2,1,0:T(2,128)(2,1)} fusion(bf16[1024,2,128]{2,1,0:T(2,128)(2,1)S(1)} %bitcast.30, s32[8192]{0:T(1024)S(1)} %fusion.23), kind=kCustom, calls=%fused_computation.2 | custom fusion | bytes 8421376 | tf_op jit(solution)/shard_map/gather | solution.py:37
  141.3 8.7 %slice_convert_fusion = (f32[8192,1,128]{2,1,0:T(1,128)S(1)}, bf16[8192,1,128]{2,1,0:T(2,128)(2,1)S(1)}) fusion(bf16[8192,2,128]{2,1,0:T(2,128)(2,1)} %gather_fusion.2), kind=kLoop, calls=%fused_computation.25 | loop fusion | flops 1048576 | bytes 10485760 | tf_op jit(solution)/shard_map/convert_element_type | solution.py:47
  150.0 0.0 copy-start.4
  150.0 0.0 copy-done.3
  150.0 0.0 copy-start.12
  150.0 0.8 fusion.3
  150.9 0.0 copy-start.5
  150.9 0.0 copy-done
  150.9 0.0 copy-start.9
  150.9 4.2 multiply_convert_fusion
  155.1 3.9 fusion.28
  159.0 2.6 fusion.11
  161.6 6.9 %fusion.13 = f32[8192,384]{1,0:T(8,128)} fusion(bf16[384,256]{1,0:T(8,128)(2,1)S(1)} %copy-done, bf16[8192,256]{1,0:T(8,128)(2,1)S(1)} %get-tuple-element.18), kind=kOutput, calls=%fused_computation.32 | convolution fusion | flops 1610612736 | bytes 16973824 | tf_op jit(solution)/shard_map/dot_general | solution.py:50
  168.5 45.7 %scatter_custom_fusion.2 = f32[1024,128]{1,0:T(8,128)} fusion(s32[8192]{0:T(1024)S(1)} %copy-done.11, bf16[8192,128]{1,0:T(8,128)(2,1)S(1)} %copy-done.3, f32[8192,384]{1,0:T(8,128)} %fusion.13, f32[]{:T(128)} %constant.11.clone.1), kind=kCustom, calls=%fused_computation.19 | custom fusion | flops 4194304 | bytes 11010560 | tf_op jit(solution)/shard_map/scatter-add | solution.py:54
  214.3 1.8 convert.12
  216.0 5.4 %fusion.29 = f32[8192,128]{1,0:T(8,128)} fusion(bf16[8192,256]{1,0:T(8,128)(2,1)} %get-tuple-element.15, bf16[256,128]{1,0:T(8,128)(2,1)S(1)} %copy-done.9), kind=kOutput, calls=%fused_computation.58 | convolution fusion | flops 536870912 | bytes 8454144 | tf_op jit(solution)/shard_map/dot_general | solution.py:46
  221.4 45.2 %scatter_custom_fusion.1 = f32[1024,128]{1,0:T(8,128)} fusion(s32[8192]{0:T(1024)S(1)} %copy-done.11, f32[8192,128]{1,0:T(8,128)} %fusion.29, f32[]{:T(128)} %constant.11.clone.1), kind=kCustom, calls=%fused_computation.43 | custom fusion | flops 1048576 | bytes 524800 | tf_op jit(solution)/shard_map/scatter-add | solution.py:53
  266.7 1.1 convert.11
  267.7 1.0 pad_maximum_fusion.4
  268.7 0.9 copy.25
  269.6 5.8 %all-to-all-start.1 = ((bf16[32,32,2,128]{3,1,2,0:T(8,128)(2,1)}), bf16[32,32,2,128]{3,1,2,0:T(8,128)(2,1)}, u32[]{:S(2)}, u32[]{:S(2)}) async-start(bf16[32,32,2,128]{3,1,2,0:T(8,128)(2,1)} %copy.25), calls=%async_computation.1 | async-start | bytes 1048576 | tf_op jit(solution)/shard_map/all_to_all | solution.py:60
  275.4 0.0 copy-start.10
  275.4 0.0 all-reduce.5.cloned.1.call-start
  275.5 5.4 %fusion.26 = f32[256,128]{1,0:T(8,128)} fusion(bf16[8192,256]{1,0:T(8,128)(2,1)} %get-tuple-element.15, f32[8192,128]{1,0:T(8,128)} %bitcast.32, bf16[8192,128]{1,0:T(8,128)(2,1)S(1)} %copy-done.7), kind=kOutput, calls=%fused_computation.55 | convolution fusion | flops 540016640 | bytes 10616832 | tf_op jit(solution)/shard_map/dot_general | solution.py:62
  280.9 0.0 all-reduce.5.cloned.1.call-update
  280.9 0.0 all-reduce.7.cloned.1.call-start
  281.0 0.1 convert_element_type.68
  281.0 0.1 reshape_squeeze.3
  281.1 0.1 convert_element_type.55
  281.2 45.5 %scatter_custom_fusion.4 = f32[2048,128]{1,0:T(8,128)S(1)} fusion(f32[2048,128]{1,0:T(8,128)S(1)} %convert_element_type.68, s32[8192]{0:T(1024)S(1)} %copy-done.8, bf16[8192,128]{1,0:T(8,128)(2,1)} %copy-done.5, f32[8192,384]{1,0:T(8,128)} %fusion.13), kind=kCustom, calls=%fused_computation.22 | custom fusion | flops 4194304 | bytes 11534336 | tf_op jit(solution)/shard_map/scatter-add | solution.py:67
  326.7 44.7 %scatter_fusion = f32[2048,128]{1,0:T(8,128)S(1)} fusion(f32[2048,128]{1,0:T(8,128)S(1)} %convert_element_type.55, s32[8192]{0:T(1024)S(1)} %copy-done.8, f32[8192,128]{1,0:T(8,128)} %fusion.29), kind=kCustom, calls=%fused_computation.4 | custom fusion | flops 1048576 | bytes 12615680 | tf_op jit(solution)/shard_map/scatter-add | solution.py:66
  371.4 21.6 %psum.44 = f32[256]{0:T(256)S(1)} all-reduce(f32[256]{0:T(256)S(1)} %get-tuple-element.17), channel_id=1, replica_groups=mesh['phi'=4,'eta'=8] {'eta'}, use_global_device_ids=true, to_apply=%region_9.10 | all-reduce | flops 256 | bytes 2048 | tf_op jit(solution)/shard_map/psum | solution.py:9
  393.0 6.2 %psum.45 = f32[256]{0:T(256)} all-reduce(f32[256]{0:T(256)S(1)} %psum.44), channel_id=1, replica_groups=mesh['phi'=4,'eta'=8] {'phi'}, use_global_device_ids=true, to_apply=%region_10.11 | all-reduce | flops 256 | bytes 2048 | tf_op jit(solution)/shard_map/psum | solution.py:10
  399.2 0.0 all-reduce.7.cloned.1.call-update
  399.2 0.0 all-to-all-done.1
  399.3 1.2 broadcast_select_fusion
  400.6 6.5 %scatter_custom_fusion.5 = f32[2048,128]{1,0:T(8,128)S(1)} fusion(f32[2048,128]{1,0:T(8,128)S(1)} %scatter_custom_fusion.4, s32[1024]{0:T(1024)S(1)} %bitcast.38, bf16[1024,128]{1,0:T(8,128)(2,1)S(1)} %bitcast.36), kind=kCustom, calls=%fused_computation.36 | custom fusion | flops 262144 | bytes 1310720 | tf_op jit(solution)/shard_map/scatter-add | solution.py:72
  407.0 0.8 convert_element_type.71
  407.9 6.5 %scatter_custom_fusion.3 = f32[2048,128]{1,0:T(8,128)S(1)} fusion(f32[2048,128]{1,0:T(8,128)S(1)} %scatter_fusion, s32[1024]{0:T(1024)S(1)} %bitcast.39, bf16[1024,128]{1,0:T(8,128)(2,1)S(1)} %bitcast.34), kind=kCustom, calls=%fused_computation.38 | custom fusion | flops 262144 | bytes 1310720 | tf_op jit(solution)/shard_map/scatter-add | solution.py:69
  414.3 0.8 convert_element_type.67
  415.2 15.2 %all-reduce.7.cloned.1.call-done = (f32[384,256]{1,0:T(8,128)}, f32[256,128]{1,0:T(8,128)}) async-done(((f32[384,256]{1,0:T(8,128)}, f32[256,128]{1,0:T(8,128)}), (f32[384,256]{1,0:T(8,128)}, f32[256,128]{1,0:T(8,128)})) %all-reduce.7.cloned.1.call-update) | async-done | bytes 524304 | tf_op jit(solution)/shard_map/psum | solution.py:10
  430.4 1.8 copy.38
  432.2 1.6 copy.39
  (17 shorter events, 0.1 us)
Async XLA Ops:
  7.2 143.7 %copy-start = (bf16[384,256]{1,0:T(8,128)(2,1)S(1)}, bf16[384,256]{1,0:T(8,128)(2,1)}, u32[]{:S(2)}) copy-start(bf16[384,256]{1,0:T(8,128)(2,1)} %param.15) | copy-start | bytes 589828
  9.7 19.3 %copy-start.8 = (s32[8192]{0:T(1024)S(1)}, s32[8192]{0:T(1024)}, u32[]{:S(2)}) copy-start(s32[8192]{0:T(1024)} %param.13) | copy-start | bytes 98308
  9.8 19.3 %copy-start.2 = (bf16[2048,128]{1,0:T(8,128)(2,1)S(1)}, bf16[2048,128]{1,0:T(8,128)(2,1)}, u32[]{:S(2)}) copy-start(bf16[2048,128]{1,0:T(8,128)(2,1)} %param.9) | copy-start | bytes 1572868
  21.6 66.0 %all-to-all-start = ((bf16[32,32,2,128]{3,1,2,0:T(8,128)(2,1)}), bf16[32,32,2,128]{3,1,2,0:T(8,128)(2,1)S(1)}, u32[]{:S(2)}, u32[]{:S(2)}) async-start(bf16[32,32,2,128]{3,1,2,0:T(8,128)(2,1)} %copy_select_fusion), calls=%async_computation | async-start | bytes 1048576 | tf_op jit(solution)/shard_map/all_to_all | solution.py:33
  29.1 29.2 %copy-start.1 = (bf16[2048,128]{1,0:T(8,128)(2,1)S(1)}, bf16[2048,128]{1,0:T(8,128)(2,1)}, u32[]{:S(2)}) copy-start(bf16[2048,128]{1,0:T(8,128)(2,1)} %param.10) | copy-start | bytes 1572868
  58.3 29.2 %copy-start.11 = (s32[8192]{0:T(1024)S(1)}, s32[8192]{0:T(1024)}, u32[]{:S(2)}) copy-start(s32[8192]{0:T(1024)} %param.14) | copy-start | bytes 98308
  141.3 8.7 %copy-start.3 = (bf16[8192,128]{1,0:T(8,128)(2,1)S(1)}, bf16[8192,128]{1,0:T(8,128)(2,1)}, u32[]{:S(2)}) copy-start(bf16[8192,128]{1,0:T(8,128)(2,1)} %gather_fusion) | copy-start | bytes 6291460
  150.0 5.1 %copy-start.4 = (f32[8192,1,128]{2,1,0:T(1,128)}, f32[8192,1,128]{2,1,0:T(1,128)S(1)}, u32[]{:S(2)}) copy-start(f32[8192,1,128]{2,1,0:T(1,128)S(1)} %get-tuple-element.11) | copy-start | bytes 12582916
  150.0 0.9 copy-start.12
  150.9 8.1 %copy-start.5 = (bf16[8192,128]{1,0:T(8,128)(2,1)}, bf16[8192,128]{1,0:T(8,128)(2,1)S(1)}, u32[]{:S(2)}) copy-start(bf16[8192,128]{1,0:T(8,128)(2,1)S(1)} %get-tuple-element.10) | copy-start | bytes 6291460
  150.9 4.2 copy-start.6
  150.9 4.2 copy-start.9
  221.4 54.0 %copy-start.7 = (bf16[8192,128]{1,0:T(8,128)(2,1)S(1)}, bf16[8192,128]{1,0:T(8,128)(2,1)}, u32[]{:S(2)}) copy-start(bf16[8192,128]{1,0:T(8,128)(2,1)} %gather_fusion.3) | copy-start | bytes 6291460
  269.6 129.7 %all-to-all-start.1 = ((bf16[32,32,2,128]{3,1,2,0:T(8,128)(2,1)}), bf16[32,32,2,128]{3,1,2,0:T(8,128)(2,1)}, u32[]{:S(2)}, u32[]{:S(2)}) async-start(bf16[32,32,2,128]{3,1,2,0:T(8,128)(2,1)} %copy.25), calls=%async_computation.1 | async-start | bytes 1048576 | tf_op jit(solution)/shard_map/all_to_all | solution.py:60
  275.4 5.6 %copy-start.10 = (s32[1,32,32]{2,1,0:T(8,128)S(1)}, s32[1,32,32]{2,1,0:T(8,128)}, u32[]{:S(2)}) copy-start(s32[1,32,32]{2,1,0:T(8,128)} %param.11) | copy-start | bytes 12292
  275.4 123.8 %all-reduce.5.cloned.1.call-start = ((), (), s32[]{:S(2)}) async-start(), calls=%async_computation.2 | async-start | bytes 1048576 | tf_op jit(solution)/shard_map/psum | solution.py:9
  280.9 149.5 %all-reduce.7.cloned.1.call-start = ((), (), s32[]{:S(2)}) async-start(), calls=%async_computation.3 | async-start | bytes 1048576 | tf_op jit(solution)/shard_map/psum | solution.py:10
Sparse Core Ops, SparseCore 0:
  281.0 73.8 all-reduce.4
  399.4 30.9 all-reduce.6
